TPU v7x, 32 devices: a whole 2x2x4 slice. The times are simulated.
32 devices in a mesh: fact: 4 (over z), dim: 8 (over y, x, core).
Axes of the slice: x: 2, y: 2, z: 4, core: 2. Of those that a mesh axis runs over, the one named last changes fastest.
Arguments:
- facts: bfloat16 [4096, 512], P(('fact', 'dim')), may hold values from -6 to 6
- dims: bfloat16 [4096, 512], P(('fact', 'dim')), may hold values from -6 to 6
- tiles: bfloat16 [1024, 128, 128], P(('fact', 'dim')), may hold values from -0.125 to 0.125
- links: int32 [1024, 2], P(('fact', 'dim')), may hold values from 0 to 31, as said below
- link_count: int32 [32], P(('fact', 'dim')), may hold values from 8 to 32, as said below
- block_table: int32 [32], replicated, may hold values from 0 to 2
- w_self: bfloat16 [512, 512], replicated, may hold values from -0.25 to 0.25
- w_tables: bfloat16 [3, 512, 512], replicated, may hold values from -0.25 to 0.25
- cot: bfloat16 [4096, 512], P(('fact', 'dim')), may hold values from -6 to 6
Outputs:
- fact_out: bfloat16 [4096, 512], P(('fact', 'dim'))
- grad_dims: float32 [4096, 512], P(('fact', 'dim'))
- grad_w_self: float32 [512, 512], replicated
- grad_w_tables: float32 [3, 512, 512], replicated
Inputs may be any that keep to these rules, and one draw needn't show every extreme that they name: On device k = f * 8 + d (f, d its fact and dim indices), links[l,0] is a fact block among those of rows f * 128 * 8 to (f + 1) * 128 * 8 - 1, and links[l,1] is a dimension block held by a device with dim index d, i.e. links[l,1] % 8 == d. Slots beyond the device's count hold such indices too and are padding. `link_count`: some device has all 32 slots live and some device exactly 8.
All inputs are finite; a program needn't handle non-finite values.
Results may differ from a plain program's by a relative error of at most 0.017.
Values may be sent and summed in bfloat16 or wider, within the bound.
A program may use at most 64 MiB of HBM per device.

v0:
```python
import math
import jax
import jax.numpy as jnp
from jax import lax
from jax.sharding import PartitionSpec as P


def project_rows(rows, row_table, w_tables):
    acc = jnp.zeros((rows.shape[0], w_tables.shape[2]), jnp.float32)
    for table in range(w_tables.shape[0]):
        term = jnp.dot(rows, w_tables[table], preferred_element_type=jnp.float32)
        acc = acc + jnp.where(row_table[:, None] == table, term, jnp.float32(0.0))
    return acc.astype(jnp.bfloat16)


def lookup_tables(global_blocks, block_table):
    every = jnp.arange(block_table.shape[0], dtype=jnp.int32)
    match = global_blocks[:, None] == every[None, :]
    return jnp.sum(jnp.where(match, block_table[None, :], 0), axis=1)


def body(facts, dims, tiles, links, link_count, block_table, w_self, w_tables, cot):
    n_fact = lax.axis_size("fact")
    n_dim = lax.axis_size("dim")
    fact_pos = lax.axis_index("fact")
    dim_pos = lax.axis_index("dim")
    block = tiles.shape[1]
    width = facts.shape[1]
    rows_own = facts.shape[0]
    dim_own = dims.shape[0]
    link_slots = tiles.shape[0]
    tables = w_tables.shape[0]
    shard_rows = rows_own * n_dim
    panel_rows = dim_own * n_fact
    per_owner = dim_own // block
    own_blocks = (fact_pos * n_dim + dim_pos) * per_owner + jnp.arange(per_owner, dtype=jnp.int32)
    own_row_table = jnp.repeat(lookup_tables(own_blocks, block_table), block)
    panel_local = jnp.arange(n_fact * per_owner, dtype=jnp.int32)
    panel_blocks_global = (
        panel_local // per_owner * n_dim + dim_pos
    ) * per_owner + panel_local % per_owner
    panel_row_table = jnp.repeat(lookup_tables(panel_blocks_global, block_table), block)
    panel = project_rows(
        lax.all_gather(dims, "fact", axis=0, tiled=True), panel_row_table, w_tables
    )
    fact_blk = links[:, 0] - fact_pos * (shard_rows // block)
    global_dim = links[:, 1]
    holder = global_dim // per_owner // n_dim
    dim_blk = holder * per_owner + global_dim % per_owner
    live = (jnp.arange(link_slots, dtype=jnp.int32) < link_count[0]).astype(jnp.float32)
    group = math.gcd(link_slots, 32)
    steps_count = link_slots // group
    tile_groups = tiles.reshape(steps_count, group, block, block)
    fact_groups = fact_blk.reshape(steps_count, group)
    dim_groups = dim_blk.reshape(steps_count, group)
    live_groups = live.reshape(steps_count, group)
    panel_blocks = panel.reshape(panel_rows // block, block, width)

    def forward_step(acc, xs):
        tile, fact_ids, dim_ids, alive = xs
        contrib = jnp.einsum(
            "lij,ljd->lid", tile, panel_blocks[dim_ids], preferred_element_type=jnp.float32
        )
        return (acc.at[fact_ids].add(contrib * alive[:, None, None]), None)

    start_fwd = jnp.zeros((shard_rows // block, block, width), jnp.float32)
    partial_value, _ = lax.scan(
        forward_step, start_fwd, (tile_groups, fact_groups, dim_groups, live_groups)
    )
    agg = lax.psum_scatter(
        partial_value.reshape(shard_rows, width).astype(jnp.bfloat16),
        "dim",
        scatter_dimension=0,
        tiled=True,
    ).astype(jnp.float32)
    pre = jnp.dot(facts, w_self, preferred_element_type=jnp.float32) + agg
    fact_out = jax.nn.silu(pre).astype(jnp.bfloat16)
    sig = jax.nn.sigmoid(pre)
    grad_pre = (cot.astype(jnp.float32) * sig * (1.0 + pre * (1.0 - sig))).astype(jnp.bfloat16)
    total_facts = rows_own * n_fact * n_dim
    total_dims = dim_own * n_fact * n_dim
    grad_self = lax.dot_general(
        facts, grad_pre, (((0,), (0,)), ((), ())), preferred_element_type=jnp.float32
    ) * total_facts ** (-0.5)
    shard_grad = lax.all_gather(grad_pre, "dim", axis=0, tiled=True)
    grad_blocks = shard_grad.reshape(shard_rows // block, block, width)

    def backward_step(acc, xs):
        tile, fact_ids, dim_ids, alive = xs
        contrib = jnp.einsum(
            "lji,ljd->lid", tile, grad_blocks[fact_ids], preferred_element_type=jnp.float32
        )
        return (acc.at[dim_ids].add(contrib * alive[:, None, None]), None)

    start_bwd = jnp.zeros((panel_rows // block, block, width), jnp.float32)
    panel_grad, _ = lax.scan(
        backward_step, start_bwd, (tile_groups, fact_groups, dim_groups, live_groups)
    )
    own_grad = lax.psum_scatter(
        panel_grad.reshape(panel_rows, width).astype(jnp.bfloat16),
        "fact",
        scatter_dimension=0,
        tiled=True,
    )
    grad_dims = jnp.zeros((dim_own, width), jnp.float32)
    table_grads = []
    for table in range(tables):
        term = lax.dot_general(
            own_grad, w_tables[table], (((1,), (1,)), ((), ())), preferred_element_type=jnp.float32
        )
        grad_dims = grad_dims + jnp.where(own_row_table[:, None] == table, term, jnp.float32(0.0))
        masked = jnp.where(own_row_table[:, None] == table, dims, jnp.zeros_like(dims))
        table_grads.append(
            lax.dot_general(
                masked, own_grad, (((0,), (0,)), ((), ())), preferred_element_type=jnp.float32
            )
            * total_dims ** (-0.5)
        )
    grad_tab = jnp.stack(table_grads)
    grad_self, grad_tab = lax.psum((grad_self, grad_tab), ("fact", "dim"))
    return (fact_out, grad_dims, grad_self, grad_tab)


def solution(mesh):
    placed = (
        P(("fact", "dim"), None),
        P(("fact", "dim"), None),
        P(("fact", "dim"), None, None),
        P(("fact", "dim"), None),
        P(("fact", "dim")),
        P(),
        P(),
        P(),
        P(("fact", "dim"), None),
    )
    return jax.shard_map(
        body,
        mesh=mesh,
        in_specs=placed,
        out_specs=(P(("fact", "dim"), None), P(("fact", "dim"), None), P(), P()),
        check_vma=False,
    )
```

profile of v0, /device:TPU:0, one launch (start us, length us, event | category | flops | bytes accessed | tf_op | source)
XLA Modules:
  0.0 342.8 jit_solution(11924869971505833211)
XLA Ops:
  8.2 17.6 %all_gather.6 = bf16[512,512]{1,0:T(8,128)(2,1)S(1)} all-gather(bf16[128,512]{1,0:T(8,128)(2,1)} %param.10), channel_id=1, replica_groups=mesh['fact'=4,'dim'=8] {'fact'}, dimensions={0}, use_global_device_ids=true | all-gather | bytes 655360 | tf_op jit(solution)/shard_map/all_gather | solution.py:44
  25.8 1.5 convolution_select_fusion
  27.3 2.5 convolution_select_fusion.1
  30.5 1.8 fusion.6
  32.4 2.8 gather_fusion
  35.2 7.1 %multiply_bitcast_fusion.1 = f32[32,128,512]{1,2,0:T(8,128)} fusion(f32[32]{0:T(128)S(1)} %compare_convert_fusion, bf16[32,128,512]{2,1,0:T(8,128)(2,1)} %gather_fusion, bf16[32,128,128]{2,1,0:T(8,128)(2,1)S(1)} %copy-done), kind=kOutput, calls=%fused_computation.5 | convolution fusion | flops 538968064 | bytes 13631616 | tf_op jit(solution)/shard_map/while/body/eval_jaxpr/lij,ljd->lid/dot_general | solution.py:61
  42.2 9.0 %copy.22 = f32[32,128,512]{2,1,0:T(8,128)} copy(f32[32,128,512]{1,2,0:T(8,128)} %multiply_bitcast_fusion.1) | data formatting | bytes 16777216 | tf_op jit(solution)/shard_map/while/body/eval_jaxpr/mul | solution.py:64
  51.5 11.8 %scatter_fusion = f32[8,128,512]{2,1,0:T(8,128)S(1)} fusion(f32[8,128,512]{2,1,0:T(8,128)S(1)} %broadcast_in_dim.107, s32[32]{0:T(128)S(1)} %get-tuple-element.63, f32[32,128,512]{2,1,0:T(8,128)} %copy.22), kind=kCustom, calls=%fused_computation.2 | custom fusion | flops 2097152 | bytes 25165952 | tf_op jit(solution)/shard_map/while/body/eval_jaxpr/scatter-add | solution.py:64
  64.5 37.8 %reduce-scatter.3.cloned.1.call-done = bf16[128,512]{1,0:T(8,128)(2,1)} async-done(((bf16[1024,512]{1,0:T(8,128)(2,1)}), bf16[128,512]{1,0:T(8,128)(2,1)}) %reduce-scatter.3.cloned.1.call-update) | async-done | bytes 131088 | tf_op jit(solution)/shard_map/reduce_scatter | solution.py:70
  102.3 2.1 multiply_convert_fusion
  104.5 23.7 %all-gather.2.cloned.1.call-done = bf16[1024,512]{1,0:T(8,128)(2,1)} async-done(((bf16[128,512]{1,0:T(8,128)(2,1)}), bf16[1024,512]{1,0:T(8,128)(2,1)}) %all-gather.2.cloned.1.call-update) | async-done | bytes 1048592 | tf_op jit(solution)/shard_map/all_gather | solution.py:85
  128.2 4.0 %gather_fusion.1 = bf16[32,128,512]{2,1,0:T(8,128)(2,1)} fusion(bf16[8,128,512]{2,1,0:T(8,128)(2,1)} %bitcast.61, s32[1024]{0:T(1024)S(1)} %pad_clamp_fusion), kind=kCustom, calls=%fused_computation.1 | custom fusion | bytes 8388736 | tf_op jit(solution)/shard_map/while/body/eval_jaxpr/gather | solution.py:91
  132.2 7.1 %multiply_bitcast_fusion = f32[32,128,512]{1,2,0:T(8,128)} fusion(f32[32]{0:T(128)S(1)} %compare_convert_fusion, bf16[32,128,512]{2,1,0:T(8,128)(2,1)} %gather_fusion.1, bf16[32,128,128]{2,1,0:T(8,128)(2,1)S(1)} %copy-done), kind=kOutput, calls=%fused_computation.4 | convolution fusion | flops 538968064 | bytes 13631616 | tf_op jit(solution)/shard_map/while/body/eval_jaxpr/lji,ljd->lid/dot_general | solution.py:90
  139.2 9.0 %copy.24 = f32[32,128,512]{2,1,0:T(8,128)} copy(f32[32,128,512]{1,2,0:T(8,128)} %multiply_bitcast_fusion) | data formatting | bytes 16777216 | tf_op jit(solution)/shard_map/while/body/eval_jaxpr/mul | solution.py:93
  148.4 11.7 %scatter_fusion.1 = f32[4,128,512]{2,1,0:T(8,128)S(1)} fusion(f32[4,128,512]{2,1,0:T(8,128)S(1)} %broadcast_in_dim.119, s32[32]{0:T(128)S(1)} %get-tuple-element.62, f32[32,128,512]{2,1,0:T(8,128)} %copy.24), kind=kCustom, calls=%fused_computation.3 | custom fusion | flops 2097152 | bytes 25165952 | tf_op jit(solution)/shard_map/while/body/eval_jaxpr/scatter-add | solution.py:93
  163.6 1.3 fusion.3
  164.9 18.1 %reduce-scatter.5.cloned.1.call-done = bf16[128,512]{1,0:T(8,128)(2,1)} async-done(((bf16[512,512]{1,0:T(8,128)(2,1)}), bf16[128,512]{1,0:T(8,128)(2,1)}) %reduce-scatter.5.cloned.1.call-update) | async-done | bytes 131088 | tf_op jit(solution)/shard_map/reduce_scatter | solution.py:99
  183.0 1.2 fusion
  184.2 1.2 fusion.1
  185.4 1.2 fusion.2
  186.7 2.0 pad_maximum_fusion
  190.3 139.5 %all-reduce.3.cloned.1.call-done = (f32[512,512]{0,1:T(8,128)}, f32[3,512,512]{2,1,0:T(8,128)}) async-done(((f32[512,512]{0,1:T(8,128)}, f32[3,512,512]{2,1,0:T(8,128)}), (f32[512,512]{0,1:T(8,128)}, f32[3,512,512]{2,1,0:T(8,128)})) %all-reduce.3.cloned.1.call-update) | async-done | bytes 4194320 | tf_op jit(solution)/shard_map/psum | solution.py:120
  329.8 2.6 copy.25
  332.4 3.9 %copy.33 = f32[3,512,512]{2,1,0:T(8,128)} copy(f32[3,512,512]{2,1,0:T(8,128)} %get-tuple-element.72) | data formatting | bytes 6291456
  (45 shorter events, 6.0 us)
Async XLA Ops:
  7.2 28.0 %copy-start = (bf16[32,128,128]{2,1,0:T(8,128)(2,1)S(1)}, bf16[32,128,128]{2,1,0:T(8,128)(2,1)}, u32[]{:S(2)}) copy-start(bf16[32,128,128]{2,1,0:T(8,128)(2,1)} %param.11) | copy-start | bytes 3145732
  7.2 22.7 %copy-start.7 = (s32[32,2]{0,1:T(2,128)S(1)}, s32[32,2]{0,1:T(2,128)}, u32[]{:S(2)}) copy-start(s32[32,2]{0,1:T(2,128)} %param.12) | copy-start | bytes 772
  7.2 95.1 %reduce-scatter.3.cloned.1.call-start = ((), (), s32[]{:S(2)}) async-start(), calls=%async_computation.2 | async-start | bytes 1179648 | tf_op jit(solution)/shard_map/reduce_scatter | solution.py:70
  63.3 39.0 %copy-start.6 = (bf16[128,512]{1,0:T(8,128)(2,1)S(1)}, bf16[128,512]{1,0:T(8,128)(2,1)}, u32[]{:S(2)}) copy-start(bf16[128,512]{1,0:T(8,128)(2,1)} %param.9) | copy-start | bytes 393220
  63.3 39.0 %copy-start.8 = (bf16[128,512]{1,0:T(8,128)(2,1)S(1)}, bf16[128,512]{1,0:T(8,128)(2,1)}, u32[]{:S(2)}) copy-start(bf16[128,512]{1,0:T(8,128)(2,1)} %param.17) | copy-start | bytes 393220
  64.4 63.7 %all-gather.2.cloned.1.call-start = ((), (), s32[]{:S(2)}) async-start(), calls=%async_computation.3 | async-start | bytes 1179648 | tf_op jit(solution)/shard_map/all_gather | solution.py:85
  104.4 78.5 %reduce-scatter.5.cloned.1.call-start = ((), (), s32[]{:S(2)}) async-start(), calls=%async_computation.4 | async-start | bytes 655360 | tf_op jit(solution)/shard_map/reduce_scatter | solution.py:99
  148.4 12.6 %copy-start.9 = (s32[32]{0:T(128)S(1)}, s32[32]{0:T(128)}, u32[]{:S(2)}) copy-start(s32[32]{0:T(128)} %param.14) | copy-start | bytes 388
  148.4 15.2 %copy-start.5 = (bf16[128,512]{1,0:T(8,128)(2,1)S(1)}, bf16[128,512]{1,0:T(8,128)(2,1)}, u32[]{:S(2)}) copy-start(bf16[128,512]{1,0:T(8,128)(2,1)} %get-tuple-element.60) | copy-start | bytes 393220
  148.4 34.6 %copy-start.4 = (bf16[128,512]{1,0:T(8,128)(2,1)S(1)}, bf16[128,512]{1,0:T(8,128)(2,1)}, u32[]{:S(2)}) copy-start(bf16[128,512]{1,0:T(8,128)(2,1)} %param.10) | copy-start | bytes 393220
  160.9 168.9 %all-reduce.3.cloned.1.call-start = ((), (), s32[]{:S(2)}) async-start(), calls=%async_computation.5 | async-start | bytes 8388608 | tf_op jit(solution)/shard_map/psum | solution.py:120
  186.7 2.0 copy-start.2
  186.7 2.0 copy-start.3
  329.8 6.5 %copy-start.1 = (bf16[32,128,128]{2,1,0:T(8,128)(2,1)S(1)}, bf16[32,128,128]{2,1,0:T(8,128)(2,1)}, u32[]{:S(2)}) copy-start(bf16[32,128,128]{2,1,0:T(8,128)(2,1)} %param.11) | copy-start | bytes 3145732
Sparse Core Ops, SparseCore 0:
  64.5 37.7 reduce-scatter.2
  104.8 23.3 all-gather.1
  161.1 21.8 reduce-scatter.4
  189.1 140.6 all-reduce.2
where the time goes:
time: 344 us; the launch traced here: 343 us
  waiting for transfers between devices  219 us (64%)
  local copies, waits for them, and re-layouts  31.8 us (9%)
  other arithmetic  29 us (8%)
  matrix products  28.6 us (8%)
  blocking collectives  17.6 us (5%)
  between operations  16.6 us (5%)
    psum x1, waiting for transfers between devices, body(): grad_self, grad_tab = lax.psum((grad_self, grad_tab), ('fact', 'dim'))  139 us
    reduce_scatter x1, waiting for transfers between devices, body(): lax.psum_scatter(partial_value.reshape(shard_rows, width).astype(jnp.bflo...  37.8 us
    all_gather x1, waiting for transfers between devices, body(): shard_grad = lax.all_gather(grad_pre, 'dim', axis=0, tiled=True)  23.7 us
    reduce_scatter x1, waiting for transfers between devices, body(): lax.psum_scatter(panel_grad.reshape(panel_rows, width).astype(jnp.bfloat1...  18.1 us
    all_gather x1, blocking collectives, body(): lax.all_gather(dims, 'fact', axis=0, tiled=True)  17.6 us
    scatter-add x1, other arithmetic, forward_step(): return (acc.at[fact_ids].add(contrib * alive[:, None, None]), None)  11.8 us
    scatter-add x1, other arithmetic, backward_step(): return (acc.at[dim_ids].add(contrib * alive[:, None, None]), None)  11.7 us
    mul x1, local copies, waits for them, and re-layouts, forward_step(): return (acc.at[fact_ids].add(contrib * alive[:, None, None]), None)  9 us
  transfers between devices with their start and end apart: 4, of which 4 were waited for; matrix products, arithmetic and copies ran while one was open for 1% of the time, Pallas kernels for 0%

commit v1 on v0

--- a/solution.py
+++ b/solution.py
@@ -117,7 +117,9 @@
             * total_dims ** (-0.5)
         )
     grad_tab = jnp.stack(table_grads)
-    grad_self, grad_tab = lax.psum((grad_self, grad_tab), ("fact", "dim"))
+    grad_self, grad_tab = lax.psum(
+        lax.psum((grad_self, grad_tab), axis_name="dim"), axis_name="fact"
+    )
     return (fact_out, grad_dims, grad_self, grad_tab)
 
 

time: 344 us -> 439 us (1.28)
  waiting for transfers between devices: 219 us -> 314 us
    psum x1 -> x2, waiting for transfers between devices: 139 us -> 235 us  [the longest x1 156 us: body(): lax.psum(lax.psum((grad_self, grad_tab), axis_name='dim'), axis_name='fact')]
  transfers between devices with their start and end apart: 4 -> 5, of which waited for: 4 -> 5; matrix products, arithmetic and copies ran while one was open for 1% -> 1% of each run, Pallas kernels for 0% -> 0%
where the time goes in v1:
time: 439 us; the launch traced here: 438 us
  waiting for transfers between devices  314 us (72%)
  local copies, waits for them, and re-layouts  31.8 us (7%)
  other arithmetic  29 us (7%)
  matrix products  28.6 us (7%)
  blocking collectives  17.6 us (4%)
  between operations  16.6 us (4%)
    psum x1, waiting for transfers between devices, body(): lax.psum(lax.psum((grad_self, grad_tab), axis_name='dim'), axis_name='fact')  156 us
    psum x1, waiting for transfers between devices, body(): lax.psum((grad_self, grad_tab), axis_name='dim')  79.2 us
    reduce_scatter x1, waiting for transfers between devices, body(): lax.psum_scatter(partial_value.reshape(shard_rows, width).astype(jnp.bflo...  37.8 us
    all_gather x1, waiting for transfers between devices, body(): shard_grad = lax.all_gather(grad_pre, 'dim', axis=0, tiled=True)  23.7 us
    reduce_scatter x1, waiting for transfers between devices, body(): lax.psum_scatter(panel_grad.reshape(panel_rows, width).astype(jnp.bfloat1...  18.1 us
    all_gather x1, blocking collectives, body(): lax.all_gather(dims, 'fact', axis=0, tiled=True)  17.6 us
    scatter-add x1, other arithmetic, forward_step(): return (acc.at[fact_ids].add(contrib * alive[:, None, None]), None)  11.8 us
    scatter-add x1, other arithmetic, backward_step(): return (acc.at[dim_ids].add(contrib * alive[:, None, None]), None)  11.7 us
  transfers between devices with their start and end apart: 5, of which 5 were waited for; matrix products, arithmetic and copies ran while one was open for 1% of the time, Pallas kernels for 0%

profile of v1, /device:TPU:0, one launch (start us, length us, event | category | flops | bytes accessed | tf_op | source)
XLA Modules:
  0.0 438.2 jit_solution(7971238284229240168)
XLA Ops:
  8.2 17.6 %all_gather.6 = bf16[512,512]{1,0:T(8,128)(2,1)S(1)} all-gather(bf16[128,512]{1,0:T(8,128)(2,1)} %param.10), channel_id=1, replica_groups=mesh['fact'=4,'dim'=8] {'fact'}, dimensions={0}, use_global_device_ids=true | all-gather | bytes 655360 | tf_op jit(solution)/shard_map/all_gather | solution.py:44
  25.8 1.5 convolution_select_fusion
  27.3 2.5 convolution_select_fusion.1
  30.5 1.8 fusion.6
  32.4 2.8 gather_fusion
  35.2 7.1 %multiply_bitcast_fusion.1 = f32[32,128,512]{1,2,0:T(8,128)} fusion(f32[32]{0:T(128)S(1)} %compare_convert_fusion, bf16[32,128,512]{2,1,0:T(8,128)(2,1)} %gather_fusion, bf16[32,128,128]{2,1,0:T(8,128)(2,1)S(1)} %copy-done), kind=kOutput, calls=%fused_computation.5 | convolution fusion | flops 538968064 | bytes 13631616 | tf_op jit(solution)/shard_map/while/body/eval_jaxpr/lij,ljd->lid/dot_general | solution.py:61
  42.2 9.0 %copy.22 = f32[32,128,512]{2,1,0:T(8,128)} copy(f32[32,128,512]{1,2,0:T(8,128)} %multiply_bitcast_fusion.1) | data formatting | bytes 16777216 | tf_op jit(solution)/shard_map/while/body/eval_jaxpr/mul | solution.py:64
  51.5 11.8 %scatter_fusion = f32[8,128,512]{2,1,0:T(8,128)S(1)} fusion(f32[8,128,512]{2,1,0:T(8,128)S(1)} %broadcast_in_dim.107, s32[32]{0:T(128)S(1)} %get-tuple-element.65, f32[32,128,512]{2,1,0:T(8,128)} %copy.22), kind=kCustom, calls=%fused_computation.2 | custom fusion | flops 2097152 | bytes 25165952 | tf_op jit(solution)/shard_map/while/body/eval_jaxpr/scatter-add | solution.py:64
  64.5 37.8 %reduce-scatter.3.cloned.1.call-done = bf16[128,512]{1,0:T(8,128)(2,1)} async-done(((bf16[1024,512]{1,0:T(8,128)(2,1)}), bf16[128,512]{1,0:T(8,128)(2,1)}) %reduce-scatter.3.cloned.1.call-update) | async-done | bytes 131088 | tf_op jit(solution)/shard_map/reduce_scatter | solution.py:70
  102.3 2.1 multiply_convert_fusion
  104.5 23.7 %all-gather.2.cloned.1.call-done = bf16[1024,512]{1,0:T(8,128)(2,1)} async-done(((bf16[128,512]{1,0:T(8,128)(2,1)}), bf16[1024,512]{1,0:T(8,128)(2,1)}) %all-gather.2.cloned.1.call-update) | async-done | bytes 1048592 | tf_op jit(solution)/shard_map/all_gather | solution.py:85
  128.2 4.0 gather_fusion.1
  132.2 7.1 %multiply_bitcast_fusion = f32[32,128,512]{1,2,0:T(8,128)} fusion(f32[32]{0:T(128)S(1)} %compare_convert_fusion, bf16[32,128,512]{2,1,0:T(8,128)(2,1)} %gather_fusion.1, bf16[32,128,128]{2,1,0:T(8,128)(2,1)S(1)} %copy-done), kind=kOutput, calls=%fused_computation.4 | convolution fusion | flops 538968064 | bytes 13631616 | tf_op jit(solution)/shard_map/while/body/eval_jaxpr/lji,ljd->lid/dot_general | solution.py:90
  139.2 9.0 %copy.24 = f32[32,128,512]{2,1,0:T(8,128)} copy(f32[32,128,512]{1,2,0:T(8,128)} %multiply_bitcast_fusion) | data formatting | bytes 16777216 | tf_op jit(solution)/shard_map/while/body/eval_jaxpr/mul | solution.py:93
  148.4 11.7 %scatter_fusion.1 = f32[4,128,512]{2,1,0:T(8,128)S(1)} fusion(f32[4,128,512]{2,1,0:T(8,128)S(1)} %broadcast_in_dim.119, s32[32]{0:T(128)S(1)} %get-tuple-element.64, f32[32,128,512]{2,1,0:T(8,128)} %copy.24), kind=kCustom, calls=%fused_computation.3 | custom fusion | flops 2097152 | bytes 25165952 | tf_op jit(solution)/shard_map/while/body/eval_jaxpr/scatter-add | solution.py:93
  163.6 1.3 fusion.3
  164.9 18.1 %reduce-scatter.5.cloned.1.call-done = bf16[128,512]{1,0:T(8,128)(2,1)} async-done(((bf16[512,512]{1,0:T(8,128)(2,1)}), bf16[128,512]{1,0:T(8,128)(2,1)}) %reduce-scatter.5.cloned.1.call-update) | async-done | bytes 131088 | tf_op jit(solution)/shard_map/reduce_scatter | solution.py:99
  184.2 1.2 fusion.1
  185.4 1.2 fusion.2
  186.6 2.0 pad_maximum_fusion
  188.7 79.2 %all-reduce.5.cloned.1.call-done = (f32[512,512]{0,1:T(8,128)}, f32[3,512,512]{2,1,0:T(8,128)}) async-done(((f32[512,512]{0,1:T(8,128)}, f32[3,512,512]{2,1,0:T(8,128)}), (f32[512,512]{0,1:T(8,128)}, f32[3,512,512]{2,1,0:T(8,128)})) %all-reduce.5.cloned.1.call-update) | async-done | bytes 4194320 | tf_op jit(solution)/shard_map/psum | solution.py:121
  269.5 155.7 %all-reduce.7.cloned.1.call-done = (f32[512,512]{0,1:T(8,128)}, f32[3,512,512]{2,1,0:T(8,128)}) async-done(((f32[512,512]{0,1:T(8,128)}, f32[3,512,512]{2,1,0:T(8,128)}), (f32[512,512]{0,1:T(8,128)}, f32[3,512,512]{2,1,0:T(8,128)})) %all-reduce.7.cloned.1.call-update) | async-done | bytes 4194320 | tf_op jit(solution)/shard_map/psum | solution.py:120
  425.2 2.6 copy.25
  427.8 3.9 copy.35
  (48 shorter events, 7.3 us)
Async XLA Ops:
  7.2 28.0 %copy-start = (bf16[32,128,128]{2,1,0:T(8,128)(2,1)S(1)}, bf16[32,128,128]{2,1,0:T(8,128)(2,1)}, u32[]{:S(2)}) copy-start(bf16[32,128,128]{2,1,0:T(8,128)(2,1)} %param.11) | copy-start | bytes 3145732
  7.2 22.7 %copy-start.7 = (s32[32,2]{0,1:T(2,128)S(1)}, s32[32,2]{0,1:T(2,128)}, u32[]{:S(2)}) copy-start(s32[32,2]{0,1:T(2,128)} %param.12) | copy-start | bytes 772
  7.2 95.1 %reduce-scatter.3.cloned.1.call-start = ((), (), s32[]{:S(2)}) async-start(), calls=%async_computation.2 | async-start | bytes 1179648 | tf_op jit(solution)/shard_map/reduce_scatter | solution.py:70
  63.3 39.0 %copy-start.6 = (bf16[128,512]{1,0:T(8,128)(2,1)S(1)}, bf16[128,512]{1,0:T(8,128)(2,1)}, u32[]{:S(2)}) copy-start(bf16[128,512]{1,0:T(8,128)(2,1)} %param.9) | copy-start | bytes 393220
  63.3 39.0 %copy-start.8 = (bf16[128,512]{1,0:T(8,128)(2,1)S(1)}, bf16[128,512]{1,0:T(8,128)(2,1)}, u32[]{:S(2)}) copy-start(bf16[128,512]{1,0:T(8,128)(2,1)} %param.17) | copy-start | bytes 393220
  64.4 63.7 %all-gather.2.cloned.1.call-start = ((), (), s32[]{:S(2)}) async-start(), calls=%async_computation.3 | async-start | bytes 1179648 | tf_op jit(solution)/shard_map/all_gather | solution.py:85
  104.4 78.5 %reduce-scatter.5.cloned.1.call-start = ((), (), s32[]{:S(2)}) async-start(), calls=%async_computation.4 | async-start | bytes 655360 | tf_op jit(solution)/shard_map/reduce_scatter | solution.py:99
  148.3 12.6 %copy-start.9 = (s32[32]{0:T(128)S(1)}, s32[32]{0:T(128)}, u32[]{:S(2)}) copy-start(s32[32]{0:T(128)} %param.14) | copy-start | bytes 388
  148.3 15.2 %copy-start.5 = (bf16[128,512]{1,0:T(8,128)(2,1)S(1)}, bf16[128,512]{1,0:T(8,128)(2,1)}, u32[]{:S(2)}) copy-start(bf16[128,512]{1,0:T(8,128)(2,1)} %get-tuple-element.62) | copy-start | bytes 393220
  148.4 34.6 %copy-start.4 = (bf16[128,512]{1,0:T(8,128)(2,1)S(1)}, bf16[128,512]{1,0:T(8,128)(2,1)}, u32[]{:S(2)}) copy-start(bf16[128,512]{1,0:T(8,128)(2,1)} %param.10) | copy-start | bytes 393220
  160.9 106.9 %all-reduce.5.cloned.1.call-start = ((), (), s32[]{:S(2)}) async-start(), calls=%async_computation.5 | async-start | bytes 8388608 | tf_op jit(solution)/shard_map/psum | solution.py:121
  188.6 79.3 %copy-start.2 = (bf16[128,512]{1,0:T(8,128)(2,1)S(1)}, bf16[128,512]{1,0:T(8,128)(2,1)}, u32[]{:S(2)}) copy-start(bf16[128,512]{1,0:T(8,128)(2,1)} %reduce-scatter.5.cloned.1.call-done) | copy-start | bytes 393220
  188.6 79.3 %copy-start.3 = (bf16[3,512,512]{2,1,0:T(8,128)(2,1)S(1)}, bf16[3,512,512]{2,1,0:T(8,128)(2,1)}, u32[]{:S(2)}) copy-start(bf16[3,512,512]{2,1,0:T(8,128)(2,1)} %param.16) | copy-start | bytes 4718596
  188.6 236.6 %all-reduce.7.cloned.1.call-start = ((), (), s32[]{:S(2)}) async-start(), calls=%async_computation.6 | async-start | bytes 8388608 | tf_op jit(solution)/shard_map/psum | solution.py:120
  425.2 6.5 %copy-start.1 = (bf16[32,128,128]{2,1,0:T(8,128)(2,1)S(1)}, bf16[32,128,128]{2,1,0:T(8,128)(2,1)}, u32[]{:S(2)}) copy-start(bf16[32,128,128]{2,1,0:T(8,128)(2,1)} %param.11) | copy-start | bytes 3145732
Sparse Core Ops, SparseCore 0:
  64.5 37.7 reduce-scatter.2
  104.8 23.3 all-gather.1
  161.0 21.8 reduce-scatter.4
  188.7 79.0 all-reduce.4
  270.1 155.0 all-reduce.6
